TPU v7x, 32 devices: a whole 2x2x4 slice. The times are simulated.
32 devices in a mesh: groups: 2 (over y), ctx: 8 (over z, x), head: 2 (over core).
Axes of the slice: x: 2, y: 2, z: 4, core: 2. Of those that a mesh axis runs over, the one named last changes fastest.
Arguments:
- queries: bfloat16 [2048, 2048], P(('groups', 'ctx'), 'head'), parts along dimension 0, may hold values from -16 to 16
- key_states: bfloat16 [2048, 1024], P(('groups', 'ctx'), 'head'), parts along dimension 0, may hold values from -16 to 16
- value_states: bfloat16 [2048, 1024], P(('groups', 'ctx'), 'head'), parts along dimension 0, may hold values from -6 to 6
- out_grad: bfloat16 [2048, 2048], P(('groups', 'ctx'), 'head'), parts along dimension 0, may hold values from -6 to 6
- doc_ids: int32 [32], P('groups'), parts along dimension 0, may hold values from 0 to 5, never falling along the last dimension, each value on 1 to 8 neighbouring positions
- int_pos: int32 [128], P('groups'), parts along dimension 0, may hold values from 0 to 127, as said below
- hidden: bfloat16 [128, 4608], P('groups', 'ctx'), parts along dimension 0, may hold values from -6 to 6
- upstream: bfloat16 [128, 4608], P('groups', 'ctx'), parts along dimension 0, may hold values from -3 to 3
- w_query: bfloat16 [4608, 2048], P('ctx', 'head'), may hold values from -0.09375 to 0.09375
- w_key: bfloat16 [4608, 1024], P('ctx', 'head'), may hold values from -0.09375 to 0.09375
- w_value: bfloat16 [4608, 1024], P('ctx', 'head'), may hold values from -0.09375 to 0.09375
- rotation: float32 [8, 4608], P(None, 'ctx'), may hold values from -0.09375 to 0.09375
- projection: float32 [8, 4608], P(None, 'ctx'), may hold values from -0.09375 to 0.09375
- rank_bias: float32 [8], replicated, may hold values from -4 to 4
Outputs:
- grad_rot: float32 [16, 4608], P('groups', 'ctx'), parts along dimension 0
- grad_proj: float32 [16, 4608], P('groups', 'ctx'), parts along dimension 0
- grad_bias: float32 [16], P('groups'), parts along dimension 0
There are 2 independent parts, one for each index of `groups`. A program takes and returns all parts, laid end to end along the dimension named above; an argument that names none is the same for every part. Nothing has to cross between parts.
Inputs may be any that keep to these rules, and one draw needn't show every extreme that they name: `doc_ids`: ids never fall along the blocks; each document covers 1 to 8 consecutive blocks, and one covers exactly 8. `int_pos`: each aligned group of 8 entries belongs to one block of 128 tokens and holds distinct token indices inside that block in rising order.
All inputs are finite; a program needn't handle non-finite values.
Results may differ from a plain program's by a relative error of at most 0.004.
The roundings to bfloat16 on the way count: a program that leaves them out, or rounds other values in their place, can miss the bound.
Values may be sent and summed in bfloat16 or wider, within the bound.
A program may use at most 64 MiB of HBM per device.

v0:
```python
import jax
import jax.numpy as jnp
from jax import lax
from jax.sharding import PartitionSpec as P

HD = 128
BLK = 64
POS_DEV = 8
scale_q = 1.0 / 12.0
soft_cap = 50.0
key_block = 512


def capping(dot_vals):
    return soft_cap * jnp.tanh(dot_vals * scale_q / soft_cap)


def doc_lookup(doc_table, block_idx):
    table_ids = jnp.arange(doc_table.shape[0], dtype=jnp.int32)
    return jnp.sum(
        jnp.where(block_idx[:, None] == table_ids[None, :], doc_table[None, :], 0), axis=1
    )


def local(
    queries,
    key_states,
    value_states,
    out_grad,
    doc_ids,
    int_pos,
    hidden,
    upstream,
    w_query,
    w_key,
    w_value,
    rotation,
    projection,
    rank_bias,
):
    tokens = queries.shape[0]
    kv_width = key_states.shape[1]
    groups_kv = kv_width // HD
    per_group = queries.shape[1] // kv_width
    pick_count = POS_DEV
    ctx_index = lax.axis_index("ctx")
    my_pos = lax.dynamic_slice_in_dim(int_pos, ctx_index * pick_count, pick_count, 0)
    query_pos = ctx_index * tokens + jnp.arange(tokens, dtype=jnp.int32)
    query_doc = doc_lookup(doc_ids, query_pos // BLK)
    pick_pos = ctx_index * tokens + my_pos
    pick_doc = doc_lookup(doc_ids, pick_pos // BLK)
    query_heads = queries.reshape(tokens, groups_kv, per_group, HD)
    grad_heads = out_grad.reshape(tokens, groups_kv, per_group, HD)
    pick_query = jnp.take(queries, my_pos, axis=0).reshape(pick_count, groups_kv, per_group, HD)
    pick_grad = jnp.take(out_grad, my_pos, axis=0).reshape(pick_count, groups_kv, per_group, HD)

    def visit_keys(running, kv_rows, first_row):
        z_total, numerator, main_sum, side_sum = running
        row_count = kv_rows.shape[0]
        key_pos = first_row + jnp.arange(row_count, dtype=jnp.int32)
        key_doc = doc_lookup(doc_ids, key_pos // BLK)
        key_heads = kv_rows[:, :kv_width].reshape(row_count, groups_kv, HD)
        value_heads = kv_rows[:, kv_width:].reshape(row_count, groups_kv, HD)
        capped = capping(
            jnp.einsum("tgqd,rgd->gqtr", query_heads, key_heads, preferred_element_type=jnp.float32)
        )
        visible = (
            (key_pos[None, :] <= query_pos[:, None])
            & (key_doc[None, :] == query_doc[:, None])
            & (key_pos[None, :] >= 0)
        )
        weights = jnp.where(visible, jnp.exp(capped), 0.0)
        z_total = z_total + jnp.sum(weights, axis=-1)
        numerator = numerator + jnp.einsum(
            "gqtr,rgd->tgqd",
            weights.astype(jnp.bfloat16),
            value_heads,
            preferred_element_type=jnp.float32,
        )
        pick_capped = capping(
            jnp.einsum("pgqd,rgd->gqpr", pick_query, key_heads, preferred_element_type=jnp.float32)
        )
        pick_visible = (
            (key_pos[None, :] <= pick_pos[:, None])
            & (key_doc[None, :] == pick_doc[:, None])
            & (key_pos[None, :] >= 0)
        )
        pick_weights = jnp.where(
            pick_visible, jnp.exp(pick_capped) * (1.0 - (pick_capped / soft_cap) ** 2), 0.0
        )
        prob_grad = jnp.einsum(
            "pgqd,rgd->gqpr", pick_grad, value_heads, preferred_element_type=jnp.float32
        )
        main_sum = main_sum + jnp.einsum(
            "gqpr,rgd->pgqd",
            (pick_weights * prob_grad).astype(jnp.bfloat16),
            key_heads,
            preferred_element_type=jnp.float32,
        )
        side_sum = side_sum + jnp.einsum(
            "gqpr,rgd->pgqd",
            pick_weights.astype(jnp.bfloat16),
            key_heads,
            preferred_element_type=jnp.float32,
        )
        return (z_total, numerator, main_sum, side_sum)

    kv_local = jnp.concatenate([key_states, value_states], axis=1)
    start_state = (
        jnp.zeros((groups_kv, per_group, tokens), jnp.float32),
        jnp.zeros((tokens, groups_kv, per_group, HD), jnp.float32),
        jnp.zeros((pick_count, groups_kv, per_group, HD), jnp.float32),
        jnp.zeros((pick_count, groups_kv, per_group, HD), jnp.float32),
    )
    running = start_state
    kv_piece = lax.all_gather(kv_local, "ctx", axis=0, tiled=True)
    row_count = kv_piece.shape[0]

    def one_block(accum_state, block_no):
        block_rows = lax.dynamic_slice_in_dim(kv_piece, block_no * key_block, key_block, 0)
        return (visit_keys(accum_state, block_rows, block_no * key_block), None)

    running, _ = lax.scan(one_block, running, jnp.arange(row_count // key_block, dtype=jnp.int32))
    z_total, numerator, main_sum, side_sum = running
    z_tok = jnp.transpose(z_total, (2, 0, 1))
    outputs = numerator / z_tok[..., None]
    row_delta = jnp.sum(grad_heads.astype(jnp.float32) * outputs, axis=-1)
    pick_z = jnp.take(z_tok, my_pos, axis=0)
    pick_delta = jnp.take(row_delta, my_pos, axis=0)
    dq_rows = (
        (scale_q * (main_sum - pick_delta[..., None] * side_sum) / pick_z[..., None])
        .reshape(pick_count, queries.shape[1])
        .astype(jnp.bfloat16)
    )
    delta_heads = jnp.transpose(row_delta, (1, 2, 0))
    picked = jnp.concatenate(
        [jnp.take(key_states, my_pos, axis=0), jnp.take(value_states, my_pos, axis=0)], axis=1
    )
    gathered = lax.all_gather(picked, "ctx", axis=0, tiled=True)
    block_rows = gathered
    row_ids = jnp.arange(pick_count * lax.axis_size("ctx"), dtype=jnp.int32)
    key_pos = row_ids // pick_count * tokens + int_pos
    row_count = block_rows.shape[0]
    key_doc = doc_lookup(doc_ids, key_pos // BLK)
    key_heads = block_rows[:, :kv_width].reshape(row_count, groups_kv, HD)
    value_heads = block_rows[:, kv_width:].reshape(row_count, groups_kv, HD)
    capped = capping(
        jnp.einsum("tgqd,rgd->gqtr", query_heads, key_heads, preferred_element_type=jnp.float32)
    )
    visible = (key_pos[None, :] <= query_pos[:, None]) & (key_doc[None, :] == query_doc[:, None])
    probs = jnp.where(visible, jnp.exp(capped), 0.0) / z_total[..., None]
    prob_grad = jnp.einsum(
        "tgqd,rgd->gqtr", grad_heads, value_heads, preferred_element_type=jnp.float32
    )
    dscore = probs * (prob_grad - delta_heads[..., None]) * (1.0 - (capped / soft_cap) ** 2)
    value_grad = jnp.einsum(
        "gqtr,tgqd->rgd", probs.astype(jnp.bfloat16), grad_heads, preferred_element_type=jnp.float32
    )
    key_grad = scale_q * jnp.einsum(
        "gqtr,tgqd->rgd",
        dscore.astype(jnp.bfloat16),
        query_heads,
        preferred_element_type=jnp.float32,
    )
    key_sums = lax.psum_scatter(
        jnp.concatenate(
            [key_grad.reshape(row_count, kv_width), value_grad.reshape(row_count, kv_width)], axis=1
        ),
        "ctx",
        scatter_dimension=0,
        tiled=True,
    )
    pos_rows = jnp.concatenate([dq_rows, key_sums.astype(jnp.bfloat16)], axis=1)
    weight_cat = jnp.concatenate([w_query, w_key, w_value], axis=1)
    partial_grad = lax.dot_general(
        lax.all_gather(pos_rows, "ctx", axis=0, tiled=True),
        weight_cat,
        (((1,), (1,)), ((), ())),
        preferred_element_type=jnp.float32,
    )
    resid_grad = lax.psum(partial_grad, "head") + upstream.astype(jnp.float32)
    hidden_wide = hidden.astype(jnp.float32)
    rank_part = jnp.dot(resid_grad, rotation.T, precision=lax.Precision.HIGHEST)
    state_part = jnp.dot(hidden_wide, (projection - rotation).T, precision=lax.Precision.HIGHEST)
    rank_grad, rank_state = lax.psum((rank_part, state_part), "ctx")
    rank_state = rank_state + rank_bias[None, :]
    grad_bias = jnp.sum(rank_grad, axis=0)
    grad_proj = jnp.dot(rank_grad.T, hidden_wide, precision=lax.Precision.HIGHEST)
    grad_rot = jnp.dot(rank_state.T, resid_grad, precision=lax.Precision.HIGHEST) - grad_proj
    return (grad_rot, grad_proj, grad_bias)


def solution(mesh):
    in_specs = (
        P(("groups", "ctx"), "head"),
        P(("groups", "ctx"), "head"),
        P(("groups", "ctx"), "head"),
        P(("groups", "ctx"), "head"),
        P("groups"),
        P("groups"),
        P("groups", "ctx"),
        P("groups", "ctx"),
        P("ctx", "head"),
        P("ctx", "head"),
        P("ctx", "head"),
        P(None, "ctx"),
        P(None, "ctx"),
        P(),
    )
    out_specs = (P("groups", "ctx"), P("groups", "ctx"), P("groups"))
    return jax.shard_map(local, mesh=mesh, in_specs=in_specs, out_specs=out_specs, check_vma=False)
```

profile of v0, /device:TPU:0, one launch (start us, length us, event | category | flops | bytes accessed | tf_op | source)
XLA Modules:
  0.0 219.9 jit_solution(13700051381468569167)
XLA Ops:
  7.3 1.1 copy.98
  8.4 1.0 copy.99
  9.4 0.7 pad_maximum_fusion
  10.3 1.1 copy.100
  11.4 0.7 compare_and_fusion.1
  12.1 1.6 gather_fusion
  13.7 0.6 gather_fusion.1
  14.5 0.6 gather_fusion.4
  15.1 0.6 gather_fusion.5
  15.9 32.5 %all_gather.10 = bf16[64,1024]{1,0:T(8,128)(2,1)S(1)} all-gather(bf16[8,1024]{1,0:T(8,128)(2,1)S(1)} %pad_maximum_fusion.3), channel_id=1, replica_groups=mesh['groups'=2,'ctx'=8,'head'=2] {'ctx'}, dimensions={0}, use_global_device_ids=true | all-gather | bytes 147456 | tf_op jit(solution)/shard_map/all_gather | solution.py:139
  49.4 15.3 %all-gather.2.cloned.1.call-done = bf16[1024,1024]{0,1:T(8,128)(2,1)} async-done(((bf16[128,1024]{0,1:T(8,128)(2,1)}), bf16[1024,1024]{0,1:T(8,128)(2,1)}) %all-gather.2.cloned.1.call-update) | async-done | bytes 2097168 | tf_op jit(solution)/shard_map/all_gather | solution.py:116
  64.7 10.2 %while.20 = (s32[]{:T(128)}, f32[4,2,128]{2,1,0:T(2,128)S(1)}, f32[128,4,2,128]{0,3,2,1:T(8,128)S(1)}, f32[8,4,2,128]{3,0,2,1:T(8,128)S(1)}, f32[8,4,2,128]{3,0,...) while((s32[]{:T(128)}, f32[4,2,128]{2,1,0:T(2,128)S(1)}, ...), condition=%wide.region_6.8_spmd.clone, body=%wide.region_3.7_spmd.clone.sunk | while | flops 305514112 | bytes 9383324 | solution.py:123
  64.7 0.6 dynamic_slice.26
  66.1 1.3 fusion.113
  68.2 0.9 fusion.115
  69.1 0.4 fusion.116
  69.8 0.6 dynamic_slice.26
  71.2 1.3 fusion.113
  73.3 0.9 fusion.115
  74.2 0.4 fusion.116
  75.6 0.7 pad_maximum_fusion.1
  76.7 0.6 gather_fusion.2
  77.2 0.6 gather_fusion.3
  78.2 57.9 %reduce-scatter.2.cloned.1.call-done = f32[8,1024]{1,0:T(8,128)} async-done(((f32[64,1024]{1,0:T(8,128)}), f32[8,1024]{1,0:T(8,128)}) %reduce-scatter.2.cloned.1.call-update) | async-done | bytes 32784 | tf_op jit(solution)/shard_map/reduce_scatter | solution.py:165
  136.1 0.8 convert_element_type.48
  136.8 30.9 %all_gather.11 = bf16[64,2048]{1,0:T(8,128)(2,1)S(1)} all-gather(bf16[8,2048]{1,0:T(8,128)(2,1)S(1)} %pad_maximum_fusion.2), channel_id=1, replica_groups=mesh['groups'=2,'ctx'=8,'head'=2] {'ctx'}, dimensions={0}, use_global_device_ids=true | all-gather | bytes 294912 | tf_op jit(solution)/shard_map/all_gather | solution.py:176
  167.8 2.8 %fusion.16 = f32[64,576]{1,0:T(8,128)} fusion(bf16[64,2048]{1,0:T(8,128)(2,1)S(1)} %all_gather.11, bf16[576,512]{1,0:T(8,128)(2,1)} %param.32, bf16[576,512]{1,0:T(8,128)(2,1)} %param.31, bf16[576,1024]{1,0:T(8,128)(2,1)S(1)} %copy-done.11), kind=kOutput, calls=%fused_computation.40 | convolution fusion | flops 158072832 | bytes 2768896 | tf_op jit(solution)/shard_map/dot_general | solution.py:175
  170.7 17.0 %all-reduce.3.cloned.1.call-done = f32[64,576]{1,0:T(8,128)} async-done(((f32[64,576]{1,0:T(8,128)}), f32[64,576]{1,0:T(8,128)}) %all-reduce.3.cloned.1.call-update) | async-done | bytes 147472 | tf_op jit(solution)/shard_map/psum | solution.py:181
  187.8 1.1 fusion.46
  188.9 21.9 %all-reduce = (f32[64,8]{0,1:T(8,128)S(1)}, f32[64,8]{0,1:T(8,128)S(1)}) all-reduce(f32[64,8]{0,1:T(8,128)S(1)} %fusion.46, f32[64,8]{0,1:T(8,128)S(1)} %convolution_bitcast_fusion.6), channel_id=1, replica_groups=mesh['groups'=2,'ctx'=8,'head'=2] {'ctx'}, use_global_device_ids=true, to_apply=%region_11.15 | all-reduce | flops 1024 | bytes 8192 | tf_op jit(solution)/shard_map/psum | solution.py:185
  211.0 0.6 reduce_sum.75
  211.6 1.8 convolution_subtract_fusion
  (86 shorter events, 5.6 us)
Async XLA Ops:
  7.2 163.4 %copy-start = (bf16[64,576]{1,0:T(8,128)(2,1)S(1)}, bf16[64,576]{1,0:T(8,128)(2,1)}, u32[]{:S(2)}) copy-start(bf16[64,576]{1,0:T(8,128)(2,1)} %param.28) | copy-start | bytes 221188
  7.2 7.3 %copy-start.3 = (bf16[128,512]{1,0:T(8,128)(2,1)S(1)}, bf16[128,512]{1,0:T(8,128)(2,1)}, u32[]{:S(2)}) copy-start(bf16[128,512]{1,0:T(8,128)(2,1)} %param.23) | copy-start | bytes 393220
  7.2 7.9 %copy-start.4 = (bf16[128,512]{1,0:T(8,128)(2,1)S(1)}, bf16[128,512]{1,0:T(8,128)(2,1)}, u32[]{:S(2)}) copy-start(bf16[128,512]{1,0:T(8,128)(2,1)} %param.24) | copy-start | bytes 393220
  7.2 41.3 %copy-start.9 = (s32[64]{0:T(128)S(1)}, s32[64]{0:T(128)}, u32[]{:S(2)}) copy-start(s32[64]{0:T(128)} %param.27) | copy-start | bytes 772
  7.2 6.5 %copy-start.1 = (bf16[128,1024]{1,0:T(8,128)(2,1)S(1)}, bf16[128,1024]{1,0:T(8,128)(2,1)}, u32[]{:S(2)}) copy-start(bf16[128,1024]{1,0:T(8,128)(2,1)} %param.25) | copy-start | bytes 786436
  7.2 41.4 %copy-start.8 = (s32[16]{0:T(128)S(1)}, s32[16]{0:T(128)}, u32[]{:S(2)}) copy-start(s32[16]{0:T(128)} %param.26) | copy-start | bytes 196
  7.2 57.4 %all-gather.2.cloned.1.call-start = ((), (), s32[]{:S(2)}) async-start(), calls=%async_computation.1 | async-start | bytes 2359296 | tf_op jit(solution)/shard_map/all_gather | solution.py:116
  10.2 125.9 %reduce-scatter.2.cloned.1.call-start = ((), (), s32[]{:S(2)}) async-start(), calls=%async_computation.2 | async-start | bytes 294912 | tf_op jit(solution)/shard_map/reduce_scatter | solution.py:165
  75.2 92.6 %copy-start.11 = (bf16[576,1024]{1,0:T(8,128)(2,1)S(1)}, bf16[576,1024]{1,0:T(8,128)(2,1)}, u32[]{:S(2)}) copy-start(bf16[576,1024]{1,0:T(8,128)(2,1)} %param.30) | copy-start | bytes 3538948
  76.3 111.5 %all-reduce.3.cloned.1.call-start = ((), (), s32[]{:S(2)}) async-start(), calls=%async_computation.3 | async-start | bytes 327680 | tf_op jit(solution)/shard_map/psum | solution.py:181
  167.8 2.8 %copy-start.5 = (f32[8,576]{1,0:T(8,128)S(1)}, f32[8,576]{1,0:T(8,128)}, u32[]{:S(2)}) copy-start(f32[8,576]{1,0:T(8,128)} %param.33) | copy-start | bytes 55300
  167.8 2.9 %copy-start.7 = (f32[8,576]{1,0:T(8,128)S(1)}, f32[8,576]{1,0:T(8,128)}, u32[]{:S(2)}) copy-start(f32[8,576]{1,0:T(8,128)} %param.34) | copy-start | bytes 55300
  167.8 20.0 %copy-start.2 = (bf16[64,576]{1,0:T(8,128)(2,1)S(1)}, bf16[64,576]{1,0:T(8,128)(2,1)}, u32[]{:S(2)}) copy-start(bf16[64,576]{1,0:T(8,128)(2,1)} %param.29) | copy-start | bytes 221188
  167.8 43.8 %copy-start.10 = (f32[8]{0:T(128)S(1)}, f32[8]{0:T(128)}, u32[]{:S(2)}) copy-start(f32[8]{0:T(128)} %param.35) | copy-start | bytes 100
  211.0 2.4 %copy-start.6 = (f32[8,576]{1,0:T(8,128)}, f32[8,576]{1,0:T(8,128)S(1)}, u32[]{:S(2)}) copy-start(f32[8,576]{1,0:T(8,128)S(1)} %fusion.65) | copy-start | bytes 55300
Sparse Core Ops, SparseCore 0:
  10.3 54.3 all-gather.1
  76.4 59.6 reduce-scatter.1
  170.7 17.0 all-reduce.2
where the time goes:
time: 220 us
  waiting for transfers between devices  90.3 us (41%)
  blocking collectives  85.3 us (39%)
  between operations  14.1 us (6%)
  local copies, waits for them, and re-layouts  12.4 us (6%)
  matrix products  10.7 us (5%)
  other arithmetic  5.58 us (3%)
    reduce_scatter x1, waiting for transfers between devices, local(): lax.psum_scatter(jnp.concatenate([key_grad.reshape(row_count, kv_width),...  57.9 us
    all_gather x1, blocking collectives, local(): gathered = lax.all_gather(picked, 'ctx', axis=0, tiled=True)  32.5 us
    all_gather x1, blocking collectives, local(): lax.all_gather(pos_rows, 'ctx', axis=0, tiled=True)  30.9 us
    psum x1, blocking collectives, local(): rank_grad, rank_state = lax.psum((rank_part, state_part), 'ctx')  21.9 us
    psum x1, waiting for transfers between devices, local(): resid_grad = lax.psum(partial_grad, 'head') + upstream.astype(jnp.float32)  17 us
    all_gather x1, waiting for transfers between devices, local(): kv_piece = lax.all_gather(kv_local, 'ctx', axis=0, tiled=True)  15.3 us
  transfers between devices with their start and end apart: 3, of which 3 were waited for; matrix products, arithmetic and copies ran while one was open for 4% of the time, Pallas kernels for 0%

commit v1 on v0

--- a/solution.py
+++ b/solution.py
@@ -9,6 +9,24 @@
 scale_q = 1.0 / 12.0
 soft_cap = 50.0
 key_block = 512
+
+
+def laid_out(blocks, dim):
+    blocks = jnp.moveaxis(blocks, 0, dim)
+    shape = blocks.shape
+    return blocks.reshape(*shape[:dim], shape[dim] * shape[dim + 1], *shape[dim + 2 :])
+
+
+def doubled(value, axis):
+    devices = lax.axis_size(axis)
+    blocks = value[None]
+    for level in range(devices.bit_length() - 1):
+        distance = 1 << level
+        received = lax.ppermute(blocks, axis, [(i, i ^ distance) for i in range(devices)])
+        both = jnp.stack([blocks, received])
+        upper = lax.axis_index(axis) >> level & 1
+        blocks = jnp.where(upper == 0, both, both[::-1]).reshape(-1, *value.shape)
+    return blocks
 
 
 def capping(dot_vals):
@@ -113,7 +131,7 @@
         jnp.zeros((pick_count, groups_kv, per_group, HD), jnp.float32),
     )
     running = start_state
-    kv_piece = lax.all_gather(kv_local, "ctx", axis=0, tiled=True)
+    kv_piece = laid_out(doubled(kv_local, "ctx"), 0)
     row_count = kv_piece.shape[0]
 
     def one_block(accum_state, block_no):

time: 220 us -> 270 us (1.23)
  waiting for transfers between devices: 90.3 us -> 112 us
  other arithmetic: 5.58 us -> 14 us
  blocking collectives: 85.3 us -> 90.8 us
  starting transfers between devices: 0.12 us -> 5.05 us
  local copies, waits for them, and re-layouts: 12.4 us -> 17.3 us
  matrix products: 10.7 us -> 14.3 us
    ppermute x0 -> x3, waiting for transfers between devices: none -> 36 us  [doubled(): lax.ppermute(blocks, axis, [(i, i ^ distance) for i in range(devices)])]
    all_gather x1 -> x0, waiting for transfers between devices: 15.3 us -> none  [local(): kv_piece = lax.all_gather(kv_local, 'ctx', axis=0, tiled=True)]
    all_gather x1, blocking collectives: 32.5 us -> 38.1 us  [local(): gathered = lax.all_gather(picked, 'ctx', axis=0, tiled=True)]
    ppermute x0 -> x3, starting transfers between devices: none -> 4.97 us  [doubled(): lax.ppermute(blocks, axis, [(i, i ^ distance) for i in range(devices)])]
    another operation x0 -> x2, local copies, waits for them, and re-layouts: none -> 3.98 us  [the longest x1 3.23 us: laid_out(): blocks.reshape(*shape[:dim], shape[dim] * shape[dim + 1], *shape[dim + 2:])]
    another operation x0 -> x4, other arithmetic: none -> 3.02 us  [doubled(): both = jnp.stack([blocks, received])]
  transfers between devices with their start and end apart: 3 -> 5, of which waited for: 3 -> 4; matrix products, arithmetic and copies ran while one was open for 4% -> 5% of each run, Pallas kernels for 0% -> 0%
where the time goes in v1:
time: 270 us; the launch traced here: 269 us
  waiting for transfers between devices  112 us (41%)
  blocking collectives  90.8 us (34%)
  local copies, waits for them, and re-layouts  17.3 us (6%)
  between operations  14.5 us (5%)
  matrix products  14.3 us (5%)
  other arithmetic  14 us (5%)
  starting transfers between devices  5.05 us (2%)
    reduce_scatter x1, waiting for transfers between devices, local(): lax.psum_scatter(jnp.concatenate([key_grad.reshape(row_count, kv_width),...  58.6 us
    all_gather x1, blocking collectives, local(): gathered = lax.all_gather(picked, 'ctx', axis=0, tiled=True)  38.1 us
    ppermute x3, waiting for transfers between devices, doubled(): lax.ppermute(blocks, axis, [(i, i ^ distance) for i in range(devices)])  36 us
    all_gather x1, blocking collectives, local(): lax.all_gather(pos_rows, 'ctx', axis=0, tiled=True)  30.9 us
    psum x1, blocking collectives, local(): rank_grad, rank_state = lax.psum((rank_part, state_part), 'ctx')  21.9 us
    psum x1, waiting for transfers between devices, local(): resid_grad = lax.psum(partial_grad, 'head') + upstream.astype(jnp.float32)  17.1 us
  transfers between devices with their start and end apart: 5, of which 4 were waited for; matrix products, arithmetic and copies ran while one was open for 5% of the time, Pallas kernels for 0%

profile of v1, /device:TPU:0, one launch (start us, length us, event | category | flops | bytes accessed | tf_op | source)
XLA Modules:
  0.0 269.3 jit_solution(13987661548030289032)
XLA Ops:
  7.2 0.9 constant_dynamic-update-slice_fusion.1
  8.2 0.9 constant_dynamic-update-slice_fusion
  9.1 3.0 %collective-permute-start = (bf16[1,128,1024]{2,1,0:T(8,128)(2,1)S(1)}, bf16[1,128,1024]{2,1,0:T(8,128)(2,1)S(1)}, u32[]{:S(2)}, u32[]{:S(2)}) collective-permute-start(bf16[1,128,1024]{2,1,0:T(8,128)(2,1)S(1)} %bitcast.189), channel_id=1, source_target_pairs={{0,2},{2,0},{4,6},{6,4},{8,10},{10,8},{12,14},{14,12},{1,3},{3,1},... | collective-permute-start | bytes 786440 | tf_op jit(solution)/shard_map/ppermute | solution.py:25
  12.1 0.7 compare_and_fusion.1
  12.8 1.5 gather_fusion.4
  14.3 1.5 gather_fusion.5
  15.9 2.5 collective-permute-done
  18.6 1.9 collective-permute-start.1
  20.6 38.1 %all_gather.6 = bf16[64,1024]{1,0:T(8,128)(2,1)S(1)} all-gather(bf16[8,1024]{1,0:T(8,128)(2,1)S(1)} %pad_maximum_fusion.5), channel_id=1, replica_groups=mesh['groups'=2,'ctx'=8,'head'=2] {'ctx'}, dimensions={0}, use_global_device_ids=true | all-gather | bytes 147456 | tf_op jit(solution)/shard_map/all_gather | solution.py:157
  59.8 0.8 copy.98
  62.1 0.8 copy.102
  63.0 0.8 copy.101
  64.7 0.9 fusion.22
  65.6 0.7 copy.99
  66.4 33.5 %collective-permute-done.2 = bf16[4,128,1024]{1,0,2:T(4,128)(2,1)} collective-permute-done((bf16[4,128,1024]{1,0,2:T(4,128)(2,1)S(1)}, bf16[4,128,1024]{1,0,2:T(4,128)(2,1)}, u32[]{:S(2)}, u32[]{:S(2)}) %collective-permute-start.2) | collective-permute-done | bytes 1048608 | tf_op jit(solution)/shard_map/ppermute | solution.py:25
  99.9 2.7 %pad_maximum_fusion = bf16[2,4,128,1024]{2,1,0,3:T(4,128)(2,1)S(1)} fusion(bf16[1,4,128,1024]{2,1,0,3:T(4,128)(2,1)} %bitcast.9, bf16[1,4,128,1024]{2,1,0,3:T(4,128)(2,1)S(1)} %copy.99), kind=kLoop, calls=%fused_computation.47 | loop fusion | flops 1048576 | bytes 4194304 | tf_op jit(solution)/shard_map/stack | solution.py:26
  102.6 2.4 reverse_select_fusion
  105.0 3.2 %reshape_reshape.3 = bf16[1024,1024]{0,1:T(8,128)(2,1)S(1)} reshape(bf16[2,4,128,1024]{2,1,0,3:T(4,128)(2,1)} %reverse_select_fusion) | data formatting | bytes 4194304 | tf_op jit(solution)/shard_map/reshape;reshape | solution.py:17
  108.3 12.5 %while.20 = (s32[]{:T(128)}, f32[4,2,128]{2,1,0:T(2,128)S(1)}, f32[128,4,2,128]{0,3,2,1:T(8,128)}, f32[8,4,2,128]{3,0,2,1:T(8,128)S(1)}, f32[8,4,2,128]{3,0,2,1:...) while((s32[]{:T(128)}, f32[4,2,128]{2,1,0:T(2,128)S(1)}, ...), condition=%wide.region_6.8_spmd.clone, body=%wide.region_3.7_spmd.clone.sunk | while | flops 305514112 | bytes 13577804 | solution.py:141
  111.4 1.9 fusion.117
  117.7 1.9 fusion.117
  120.9 1.3 multiply_reduce_fusion
  122.1 1.2 convolution_bitcast_fusion.4
  123.8 0.7 pad_maximum_fusion.3
  126.7 58.6 %reduce-scatter.2.cloned.1.call-done = f32[8,1024]{1,0:T(8,128)} async-done(((f32[64,1024]{1,0:T(8,128)}), f32[8,1024]{1,0:T(8,128)}) %reduce-scatter.2.cloned.1.call-update) | async-done | bytes 32784 | tf_op jit(solution)/shard_map/reduce_scatter | solution.py:183
  185.3 0.8 convert_element_type.48
  186.1 30.9 %all_gather.7 = bf16[64,2048]{1,0:T(8,128)(2,1)S(1)} all-gather(bf16[8,2048]{1,0:T(8,128)(2,1)S(1)} %pad_maximum_fusion.4), channel_id=1, replica_groups=mesh['groups'=2,'ctx'=8,'head'=2] {'ctx'}, dimensions={0}, use_global_device_ids=true | all-gather | bytes 294912 | tf_op jit(solution)/shard_map/all_gather | solution.py:194
  217.0 2.6 fusion.16
  219.8 17.1 %all-reduce.3.cloned.1.call-done = f32[64,576]{1,0:T(8,128)} async-done(((f32[64,576]{1,0:T(8,128)}), f32[64,576]{1,0:T(8,128)}) %all-reduce.3.cloned.1.call-update) | async-done | bytes 147472 | tf_op jit(solution)/shard_map/psum | solution.py:199
  236.9 1.1 fusion.48
  238.0 21.9 %all-reduce = (f32[64,8]{0,1:T(8,128)S(1)}, f32[64,8]{0,1:T(8,128)S(1)}) all-reduce(f32[64,8]{0,1:T(8,128)S(1)} %fusion.48, f32[64,8]{0,1:T(8,128)S(1)} %convolution_bitcast_fusion.6), channel_id=1, replica_groups=mesh['groups'=2,'ctx'=8,'head'=2] {'ctx'}, use_global_device_ids=true, to_apply=%region_11.15 | all-reduce | flops 1024 | bytes 8192 | tf_op jit(solution)/shard_map/psum | solution.py:203
  260.7 1.8 convolution_subtract_fusion
  (129 shorter events, 14.5 us)
Async XLA Ops:
  7.2 212.5 %copy-start = (bf16[64,576]{1,0:T(8,128)(2,1)S(1)}, bf16[64,576]{1,0:T(8,128)(2,1)}, u32[]{:S(2)}) copy-start(bf16[64,576]{1,0:T(8,128)(2,1)} %param.28) | copy-start | bytes 221188
  7.2 13.3 %copy-start.18 = (s32[64]{0:T(128)S(1)}, s32[64]{0:T(128)}, u32[]{:S(2)}) copy-start(s32[64]{0:T(128)} %param.27) | copy-start | bytes 772
  7.2 51.5 %copy-start.13 = (s32[16]{0:T(128)S(1)}, s32[16]{0:T(128)}, u32[]{:S(2)}) copy-start(s32[16]{0:T(128)} %param.26) | copy-start | bytes 196
  7.2 178.1 %reduce-scatter.2.cloned.1.call-start = ((), (), s32[]{:S(2)}) async-start(), calls=%async_computation.1 | async-start | bytes 294912 | tf_op jit(solution)/shard_map/reduce_scatter | solution.py:183
  9.1 9.3 %collective-permute-start = (bf16[1,128,1024]{2,1,0:T(8,128)(2,1)S(1)}, bf16[1,128,1024]{2,1,0:T(8,128)(2,1)S(1)}, u32[]{:S(2)}, u32[]{:S(2)}) collective-permute-start(bf16[1,128,1024]{2,1,0:T(8,128)(2,1)S(1)} %bitcast.189), channel_id=1, source_target_pairs={{0,2},{2,0},{4,6},{6,4},{8,10},{10,8},{12,14},{14,12},{1,3},{3,1},... | collective-permute-start | bytes 786440 | tf_op jit(solution)/shard_map/ppermute | solution.py:25
  12.8 51.8 %copy-start.15 = (pred[8]{0:T(512)(128)(4,1)}, pred[8]{0:T(512)(128)(4,1)S(1)}, u32[]{:S(2)}) copy-start(pred[8]{0:T(512)(128)(4,1)S(1)} %get-tuple-element.405) | copy-start | bytes 28
  12.8 48.7 %copy-start.14 = (s32[1024]{0:T(1024)}, s32[1024]{0:T(1024)S(1)}, u32[]{:S(2)}) copy-start(s32[1024]{0:T(1024)S(1)} %pad_clamp_fusion) | copy-start | bytes 12292
  18.6 40.8 %collective-permute-start.1 = (bf16[2,128,1024]{2,1,0:T(8,128)(2,1)S(1)}, bf16[2,128,1024]{2,1,0:T(8,128)(2,1)S(1)}, u32[]{:S(2)}, u32[]{:S(2)}) collective-permute-start(bf16[2,128,1024]{2,1,0:T(8,128)(2,1)S(1)} %get-tuple-element.414), channel_id=1, source_target_pairs={{0,4},{2,6},{4,0},{6,2},{8,12},{10,14},{12,8},{14,10},{1,5},{3,7},... | collective-permute-start | bytes 1572872 | tf_op jit(solution)/shard_map/ppermute | solution.py:25
  59.5 1.2 copy-start.6
  59.5 2.0 copy-start.7
  60.6 39.3 %collective-permute-start.2 = (bf16[4,128,1024]{1,0,2:T(4,128)(2,1)S(1)}, bf16[4,128,1024]{1,0,2:T(4,128)(2,1)}, u32[]{:S(2)}, u32[]{:S(2)}) collective-permute-start(bf16[4,128,1024]{1,0,2:T(4,128)(2,1)S(1)} %copy.98), channel_id=1, source_target_pairs={{0,8},{2,10},{4,12},{6,14},{8,0},{10,2},{12,4},{14,6},{1,9},{3,11}... | collective-permute-start | bytes 3145736 | tf_op jit(solution)/shard_map/ppermute | solution.py:25
  61.5 4.1 %copy-start.3 = (bf16[128,1024]{0,1:T(8,128)(2,1)}, bf16[128,1024]{0,1:T(8,128)(2,1)S(1)}, u32[]{:S(2)}) copy-start(bf16[128,1024]{0,1:T(8,128)(2,1)S(1)} %copy.100) | copy-start | bytes 786436
  108.3 1.5 copy-start.22
  111.4 1.9 copy-start.1
  113.3 1.2 copy-start.23
  113.7 0.8 copy-start.2
  114.6 1.5 copy-start.22
  117.7 1.9 copy-start.1
  119.6 1.2 copy-start.23
  120.8 2.6 copy-start.4
  120.9 2.6 copy-start.5
  120.9 2.6 copy-start.9
  120.9 2.6 copy-start.17
  123.4 2.9 %copy-start.16 = (pred[8]{0:T(512)(128)(4,1)S(1)}, pred[8]{0:T(512)(128)(4,1)}, u32[]{:S(2)}) copy-start(pred[8]{0:T(512)(128)(4,1)} %copy-done.15) | copy-start | bytes 28
  123.4 93.6 %copy-start.20 = (bf16[576,1024]{1,0:T(8,128)(2,1)S(1)}, bf16[576,1024]{1,0:T(8,128)(2,1)}, u32[]{:S(2)}) copy-start(bf16[576,1024]{1,0:T(8,128)(2,1)} %param.30) | copy-start | bytes 3538948
  123.4 93.5 %copy-start.21 = (bf16[576,512]{1,0:T(8,128)(2,1)S(1)}, bf16[576,512]{1,0:T(8,128)(2,1)}, u32[]{:S(2)}) copy-start(bf16[576,512]{1,0:T(8,128)(2,1)} %param.32) | copy-start | bytes 1769476
  124.6 112.3 %all-reduce.3.cloned.1.call-start = ((), (), s32[]{:S(2)}) async-start(), calls=%async_computation.2 | async-start | bytes 327680 | tf_op jit(solution)/shard_map/psum | solution.py:199
  217.0 2.7 copy-start.10
  217.0 2.7 copy-start.12
  217.0 19.9 %copy-start.8 = (bf16[64,576]{1,0:T(8,128)(2,1)S(1)}, bf16[64,576]{1,0:T(8,128)(2,1)}, u32[]{:S(2)}) copy-start(bf16[64,576]{1,0:T(8,128)(2,1)} %param.29) | copy-start | bytes 221188
  217.0 43.7 %copy-start.19 = (f32[8]{0:T(128)S(1)}, f32[8]{0:T(128)}, u32[]{:S(2)}) copy-start(f32[8]{0:T(128)} %param.35) | copy-start | bytes 100
  260.1 2.4 copy-start.11
  (1 other events, 0.8 us)
Sparse Core Ops, SparseCore 0:
  124.7 60.5 reduce-scatter.1
  219.8 17.0 all-reduce.2
